TPU v7x, 32 devices: a whole 2x2x4 slice. The times are simulated.
32 devices in a mesh: cuts: 2 (over y), idx: 8 (over z, x), half: 2 (over core).
Axes of the slice: x: 2, y: 2, z: 4, core: 2. Of those that a mesh axis runs over, the one named last changes fastest.
Arguments:
- left_factor: float32 [2, 4, 64, 1024, 256], P('half', 'cuts', 'idx'), parts along dimension 1, may hold values from -6 to 6
- right_factor: float32 [2, 4, 64, 256, 1024], P('half', 'cuts', None, 'idx'), parts along dimension 1, may hold values from -0.25 to 0.25
Outputs:
- amplitudes: float32 [1024, 4, 1024], P(('idx', 'half'), 'cuts'), parts along dimension 1
There are 2 independent parts, one for each index of `cuts`. A program takes and returns all parts, laid end to end along the dimension named above; each array names one. Nothing has to cross between parts.
All inputs are finite; a program needn't handle non-finite values.
Results may differ from a plain program's by a relative error of at most 0.0003.
Values sent between devices are 32-bit elements; how exact they have to be, the bound alone decides.
A program may use at most 256 MiB of HBM per device.

v0:
```python
import math
import jax
import jax.numpy as jnp
from jax import lax
from jax.sharding import PartitionSpec as P

BATCH = 64
N = 1024


def swapped(x, axis, bit):
    return lax.ppermute(x, axis, [(i, i ^ 1 << bit) for i in range(lax.axis_size(axis))])


def complex_product(left_real, left_imag, right_real, right_imag, pattern):
    highest = lax.Precision.HIGHEST
    first_term = jnp.einsum(pattern, left_real, right_real, precision=highest)
    second_term = jnp.einsum(pattern, left_imag, right_imag, precision=highest)
    mixed_term = jnp.einsum(
        pattern, left_real + left_imag, right_real + right_imag, precision=highest
    )
    return (first_term - second_term, mixed_term - first_term - second_term)


def on_device(left_factor, right_factor):
    left_local = left_factor[0]
    right_local = right_factor[0]
    columns = lax.all_to_all(right_local, "idx", split_axis=1, concat_axis=2, tiled=True)
    real_part, imag_part = complex_product(
        left_local[0], left_local[1], columns[0], columns[1], "bmk,bkn->bmn"
    )
    merged = jnp.stack([real_part, imag_part])
    half_cols = merged.shape[3] // 2
    half_index = lax.axis_index("half")
    outgoing = lax.dynamic_slice_in_dim(merged, (1 - half_index) * half_cols, half_cols, 3)
    own_slab = lax.dynamic_slice_in_dim(merged, half_index * half_cols, half_cols, 3)
    other_slab = swapped(outgoing, "half", 0)
    is_lower = half_index == 0
    first_pair = jnp.where(is_lower, own_slab, other_slab)
    second_pair = jnp.where(is_lower, other_slab, own_slab)
    norm_scale = 1.0 / math.sqrt(2.0 * BATCH * N)
    real_part, imag_part = complex_product(
        first_pair[0], first_pair[1], second_pair[0], second_pair[1], "bmn,bon->mo"
    )
    return lax.psum_scatter(
        jnp.stack([real_part, imag_part], axis=1) * norm_scale,
        ("idx", "half"),
        scatter_dimension=0,
        tiled=True,
    )


def solution(mesh):
    return jax.shard_map(
        on_device,
        mesh=mesh,
        in_specs=(P("half", "cuts", "idx", None, None), P("half", "cuts", None, "idx", None)),
        out_specs=P(("idx", "half"), "cuts", None),
        check_vma=False,
    )
```

profile of v0, /device:TPU:0, one launch (start us, length us, event | category | flops | bytes accessed | tf_op | source)
XLA Modules:
  0.0 989.9 jit_solution(9931853911004770356)
XLA Ops:
  6.5 11.8 %copy.11 = f32[1,2,64,32,1024]{4,3,1,2,0:T(8,128)} copy(f32[1,2,64,32,1024]{4,3,2,1,0:T(8,128)} %param.3) | data formatting | bytes 33554432 | tf_op args[1]
  18.3 7.3 all-to-all-start
  25.6 0.0 reduce-scatter.2.cloned.1.call-start
  25.7 363.0 %all-to-all-done = f32[2,64,32,1024]{3,2,0,1:T(8,128)} async-done(((f32[2,64,32,1024]{3,2,0,1:T(8,128)}), f32[2,64,32,1024]{3,2,0,1:T(8,128)}, u32[]{:S(2)}, u32[]{:S(2)}) %all-to-all-start) | async-done | bytes 16777248 | tf_op jit(solution)/shard_map/all_to_all | solution.py:28
  388.7 11.8 %copy.10 = f32[2,8,8,32,1024]{4,3,1,2,0:T(8,128)} copy(f32[2,8,8,32,1024]{4,3,0,2,1:T(8,128)} %bitcast.2) | data formatting | bytes 33554432 | tf_op jit(solution)/shard_map/all_to_all | solution.py:28
  400.5 6.7 fusion.38
  407.2 0.0 copy-start.1
  407.2 0.0 copy-start
  407.3 34.2 %fusion.24 = f32[8,1024,1024]{2,1,0:T(8,128)} fusion(f32[8,256,1024]{2,1,0:T(8,128)S(1)} %bitcast.103, f32[1,2,8,1024,256]{4,3,2,1,0:T(8,128)} %param.2), kind=kOutput, calls=%fused_computation.36 | convolution fusion | flops 25769803776 | bytes 50331648 | tf_op jit(solution)/shard_map/bmk,bkn->bmn/dot_general | solution.py:17
  441.5 0.0 copy-done.1
  441.5 0.0 copy-done
  441.5 32.8 %fusion.21 = f32[8,1024,1024]{2,1,0:T(8,128)} fusion(f32[8,256,1024]{2,1,0:T(8,128)S(1)} %bitcast.101, f32[1,2,8,1024,256]{4,3,2,1,0:T(8,128)} %param.2), kind=kOutput, calls=%fused_computation.33 | convolution fusion | flops 25769803776 | bytes 50331648 | tf_op jit(solution)/shard_map/bmk,bkn->bmn/dot_general | solution.py:18
  474.3 55.7 %subtract_bitcast_fusion = f32[1,8,1024,1024]{3,2,1,0:T(8,128)} fusion(f32[8,1024,1024]{2,1,0:T(8,128)} %fusion.21, f32[8,1024,1024]{2,1,0:T(8,128)} %fusion.24, f32[8,256,1024]{2,1,0:T(8,128)} %bitcast.104, f32[8,256,1024]{2,1,0:T(8,128)} %bitcast.102, f32[1,2,8,1024,256]{4,3,2,1,0:T(8,128)} %param.2), kind=kOutput, calls=%fused_computation.6 | convolution fusion | flops 25790775296 | bytes 134217728 | tf_op jit(solution)/shard_map/bmk,bkn->bmn/dot_general | solution.py:19
  530.0 33.0 %subtract_bitcast_fusion.1 = f32[1,8,1024,1024]{3,2,1,0:T(8,128)} fusion(f32[8,1024,1024]{2,1,0:T(8,128)} %fusion.24, f32[8,1024,1024]{2,1,0:T(8,128)} %fusion.21), kind=kLoop, calls=%fused_computation.7 | loop fusion | flops 8388608 | bytes 100663296 | tf_op jit(solution)/shard_map/stack | solution.py:32
  563.0 23.0 %fusion = f32[2,8,1024,512]{3,2,1,0:T(8,128)} fusion(s32[]{:T(128)S(6)} %select_n.20, f32[1,8,1024,1024]{3,2,1,0:T(8,128)} %subtract_bitcast_fusion.1, f32[1,8,1024,1024]{3,2,1,0:T(8,128)} %subtract_bitcast_fusion), kind=kLoop, calls=%fused_computation.4 | loop fusion | flops 8388608 | bytes 100663296 | tf_op jit(solution)/shard_map/stack | solution.py:32
  586.0 0.0 collective-permute-start
  586.0 49.5 %collective-permute-done = f32[2,8,1024,512]{3,2,1,0:T(8,128)} collective-permute-done((f32[2,8,1024,512]{3,2,1,0:T(8,128)}, f32[2,8,1024,512]{3,2,1,0:T(8,128)}, u32[]{:S(2)}, u32[]{:S(2)}) %collective-permute-start) | collective-permute-done | bytes 33554464 | tf_op jit(solution)/shard_map/ppermute | solution.py:12
  635.5 54.2 %broadcast_select_fusion.1 = (f32[2,8,1024,512]{3,2,1,0:T(8,128)}, f32[2,8,1024,512]{3,2,1,0:T(8,128)}) fusion(f32[2,8,1024,512]{3,2,1,0:T(8,128)} %collective-permute-done, pred[]{:T(512)S(6)} %eq.3, s32[]{:T(128)S(6)} %select_n.19, f32[1,8,1024,1024]{3,2,1,0:T(8,128)} %subtract_bitcast_fusion, f32[1,8,1024,1024]{3,2,1,0:T(8,128)} %subtract_bitcast_fusion.1), kind=kLoop, calls=%fused_computation.22 | loop fusion | flops 33554432 | bytes 167772160 | tf_op jit(solution)/shard_map/jit(_where)/select_n | solution.py:39
  689.7 59.4 %fusion.5 = f32[1024,1024,1]{1,0,2:T(8,128)S(1)} fusion(f32[2,8,1024,512]{3,2,1,0:T(8,128)} %get-tuple-element.6, f32[2,8,1024,512]{3,2,1,0:T(8,128)} %get-tuple-element.5), kind=kOutput, calls=%fused_computation.11 | convolution fusion | flops 51539607552 | bytes 37748736 | tf_op jit(solution)/shard_map/bmn,bon->mo/dot_general | solution.py:18
  749.1 59.3 %fusion.8 = f32[1024,1024,1]{1,0,2:T(8,128)S(1)} fusion(f32[2,8,1024,512]{3,2,1,0:T(8,128)} %get-tuple-element.6, f32[2,8,1024,512]{3,2,1,0:T(8,128)} %get-tuple-element.5), kind=kOutput, calls=%fused_computation.14 | convolution fusion | flops 51539607552 | bytes 37748736 | tf_op jit(solution)/shard_map/bmn,bon->mo/dot_general | solution.py:17
  808.4 63.7 %fusion.32 = f32[1024,1,1024]{2,0,1:T(8,128)S(1)} fusion(f32[1024,1024,1]{1,0,2:T(8,128)S(1)} %fusion.5, f32[1024,1024,1]{1,0,2:T(8,128)S(1)} %fusion.8, f32[2,8,1024,512]{3,2,1,0:T(8,128)} %get-tuple-element.6, f32[2,8,1024,512]{3,2,1,0:T(8,128)} %get-tuple-element.5), kind=kOutput, calls=%fused_computation.45 | convolution fusion | flops 51550093312 | bytes 79691776 | tf_op jit(solution)/shard_map/bmn,bon->mo/dot_general | solution.py:19
  872.1 1.4 fusion.33
  873.5 4.3 maximum_multiply_fusion
  877.7 0.0 reduce-scatter.2.cloned.1.call-update
  877.8 102.6 %reduce-scatter.2.cloned.1.call-done = f32[64,2,1024]{2,0,1:T(8,128)} async-done(((f32[1024,2,1024]{2,0,1:T(8,128)}), f32[64,2,1024]{2,0,1:T(8,128)}) %reduce-scatter.2.cloned.1.call-update) | async-done | bytes 524304 | tf_op jit(solution)/shard_map/reduce_scatter | solution.py:45
  980.4 2.2 copy.7
Async XLA Ops:
  18.3 370.3 %all-to-all-start = ((f32[2,64,32,1024]{3,2,0,1:T(8,128)}), f32[2,64,32,1024]{3,2,0,1:T(8,128)}, u32[]{:S(2)}, u32[]{:S(2)}) async-start(f32[2,64,32,1024]{3,2,0,1:T(8,128)} %bitcast.105), calls=%async_computation | async-start | bytes 33554432 | tf_op jit(solution)/shard_map/all_to_all | solution.py:28
  25.6 954.7 %reduce-scatter.2.cloned.1.call-start = ((), (), s32[]{:S(2)}) async-start(), calls=%async_computation.2 | async-start | bytes 8912896 | tf_op jit(solution)/shard_map/reduce_scatter | solution.py:45
  407.2 34.3 %copy-start.1 = (f32[1,8,8,32,1024]{4,3,2,1,0:T(8,128)}, f32[1,8,8,32,1024]{4,3,2,1,0:T(8,128)S(1)}, u32[]{:S(2)}) copy-start(f32[1,8,8,32,1024]{4,3,2,1,0:T(8,128)S(1)} %get-tuple-element.8) | copy-start | bytes 25165828
  407.2 34.3 %copy-start = (f32[1,8,8,32,1024]{4,3,2,1,0:T(8,128)}, f32[1,8,8,32,1024]{4,3,2,1,0:T(8,128)S(1)}, u32[]{:S(2)}) copy-start(f32[1,8,8,32,1024]{4,3,2,1,0:T(8,128)S(1)} %get-tuple-element.7) | copy-start | bytes 25165828
  586.0 49.5 %collective-permute-start = (f32[2,8,1024,512]{3,2,1,0:T(8,128)}, f32[2,8,1024,512]{3,2,1,0:T(8,128)}, u32[]{:S(2)}, u32[]{:S(2)}) collective-permute-start(f32[2,8,1024,512]{3,2,1,0:T(8,128)} %fusion), channel_id=1, source_target_pairs={{0,1},{1,0},{2,3},{3,2},{4,5},{5,4},{6,7},{7,6},{8,9},{9,8},{10,11... | collective-permute-start | bytes 100663304 | tf_op jit(solution)/shard_map/ppermute | solution.py:12
Sparse Core Ops, SparseCore 0:
  877.9 102.4 reduce-scatter.1
where the time goes:
time: 997 us; the launch traced here: 990 us
  waiting for transfers between devices  515 us (52%)
  matrix products  305 us (31%)
  other arithmetic  116 us (12%)
  local copies, waits for them, and re-layouts  32.6 us (3%)
  between operations  13.9 us (1%)
    all_to_all x1, waiting for transfers between devices, on_device(): lax.all_to_all(right_local, 'idx', split_axis=1, concat_axis=2, tiled=True)  363 us
    dot_general x2, matrix products, complex_product(): jnp.einsum(pattern, left_real + left_imag, right_real + right_imag, preci...  119 us
    reduce_scatter x1, waiting for transfers between devices, on_device(): lax.psum_scatter(jnp.stack([real_part, imag_part], axis=1) * norm_scale,...  103 us
    dot_general x2, matrix products, complex_product(): first_term = jnp.einsum(pattern, left_real, right_real, precision=highest)  93.6 us
    dot_general x2, matrix products, complex_product(): second_term = jnp.einsum(pattern, left_imag, right_imag, precision=highest)  92.2 us
    another operation x2, other arithmetic, on_device(): merged = jnp.stack([real_part, imag_part])  56 us
    select_n x1, other arithmetic, on_device(): first_pair = jnp.where(is_lower, own_slab, other_slab)  54.2 us
    ppermute x1, waiting for transfers between devices, swapped(): lax.ppermute(x, axis, [(i, i ^ 1 << bit) for i in range(lax.axis_size(axi...  49.5 us
  transfers between devices with their start and end apart: 3, of which 3 were waited for; matrix products, arithmetic and copies ran while one was open for 0% of the time, Pallas kernels for 0%

commit v1 on v0

--- a/solution.py
+++ b/solution.py
@@ -25,7 +25,10 @@
 def on_device(left_factor, right_factor):
     left_local = left_factor[0]
     right_local = right_factor[0]
-    columns = lax.all_to_all(right_local, "idx", split_axis=1, concat_axis=2, tiled=True)
+    peers = lax.axis_size("idx")
+    blocks = jnp.stack(jnp.split(right_local, peers, axis=1), axis=0)
+    blocks = lax.all_to_all(blocks, "idx", split_axis=0, concat_axis=0)
+    columns = jnp.concatenate(blocks, axis=2)
     real_part, imag_part = complex_product(
         left_local[0], left_local[1], columns[0], columns[1], "bmk,bkn->bmn"
     )

time: 997 us -> 1070 us (1.073)
  matrix products: 305 us -> 367 us
    dot_general x2, matrix products: 92.2 us -> 126 us  [complex_product(): second_term = jnp.einsum(pattern, left_imag, right_imag, precision=highest)]
    dot_general x2, matrix products: 93.6 us -> 124 us  [complex_product(): first_term = jnp.einsum(pattern, left_real, right_real, precision=highest)]
where the time goes in v1:
time: 1070 us; the launch traced here: 1060 us
  waiting for transfers between devices  515 us (48%)
  matrix products  367 us (34%)
  other arithmetic  118 us (11%)
  local copies, waits for them, and re-layouts  40.5 us (4%)
  between operations  13.7 us (1%)
    all_to_all x1, waiting for transfers between devices, on_device(): blocks = lax.all_to_all(blocks, 'idx', split_axis=0, concat_axis=0)  363 us
    dot_general x2, matrix products, complex_product(): second_term = jnp.einsum(pattern, left_imag, right_imag, precision=highest)  126 us
    dot_general x2, matrix products, complex_product(): first_term = jnp.einsum(pattern, left_real, right_real, precision=highest)  124 us
    dot_general x2, matrix products, complex_product(): jnp.einsum(pattern, left_real + left_imag, right_real + right_imag, preci...  117 us
    reduce_scatter x1, waiting for transfers between devices, on_device(): lax.psum_scatter(jnp.stack([real_part, imag_part], axis=1) * norm_scale,...  103 us
    another operation x2, other arithmetic, on_device(): merged = jnp.stack([real_part, imag_part])  56.5 us
    select_n x1, other arithmetic, on_device(): first_pair = jnp.where(is_lower, own_slab, other_slab)  56.2 us
    ppermute x1, waiting for transfers between devices, swapped(): lax.ppermute(x, axis, [(i, i ^ 1 << bit) for i in range(lax.axis_size(axi...  49.5 us
  transfers between devices with their start and end apart: 3, of which 3 were waited for; matrix products, arithmetic and copies ran while one was open for 0% of the time, Pallas kernels for 0%

profile of v1, /device:TPU:0, one launch (start us, length us, event | category | flops | bytes accessed | tf_op | source)
XLA Modules:
  0.0 1062.0 jit_solution(4471487021576950861)
XLA Ops:
  6.5 0.0 copy-start.2
  6.5 3.3 fusion.47
  9.9 3.9 fusion.46
  13.8 3.5 fusion.45
  17.2 3.2 fusion.44
  20.4 0.0 copy-done.2
  20.4 1.5 fusion.43
  21.9 1.5 fusion.42
  23.4 1.5 fusion.41
  24.9 1.4 fusion.40
  26.3 7.3 all-to-all-start
  33.6 0.0 reduce-scatter.2.cloned.1.call-start
  33.6 363.0 %all-to-all-done = f32[8,2,8,32,1024]{4,3,2,1,0:T(8,128)} async-done(((f32[8,2,8,32,1024]{4,3,2,1,0:T(8,128)}), f32[8,2,8,32,1024]{4,3,2,1,0:T(8,128)}, u32[]{:S(2)}, u32[]{:S(2)}) %all-to-all-start) | async-done | bytes 16777248 | tf_op jit(solution)/shard_map/all_to_all | solution.py:30
  396.6 11.8 %copy.52 = f32[8,2,8,32,1024]{4,3,0,2,1:T(8,128)} copy(f32[8,2,8,32,1024]{4,3,2,1,0:T(8,128)} %all-to-all-done) | data formatting | bytes 33554432 | tf_op jit(solution)/shard_map/all_to_all | solution.py:30
  408.5 6.7 fusion.48
  415.2 0.0 copy-start.1
  415.2 0.0 copy-start
  415.2 63.1 %fusion.23 = f32[8,1024,1024]{2,1,0:T(8,128)} fusion(f32[8,256,1024]{2,1,0:T(8,128)S(1)} %bitcast.148, f32[1,2,8,1024,256]{4,3,2,1,0:T(8,128)} %param.2), kind=kOutput, calls=%fused_computation.35 | convolution fusion | flops 25769803776 | bytes 50331648 | tf_op jit(solution)/shard_map/bmk,bkn->bmn/dot_general | solution.py:18
  478.3 0.0 copy-done.1
  478.3 0.0 copy-done
  478.3 61.5 %fusion.26 = f32[8,1024,1024]{2,1,0:T(8,128)} fusion(f32[8,256,1024]{2,1,0:T(8,128)S(1)} %bitcast.146, f32[1,2,8,1024,256]{4,3,2,1,0:T(8,128)} %param.2), kind=kOutput, calls=%fused_computation.38 | convolution fusion | flops 25769803776 | bytes 50331648 | tf_op jit(solution)/shard_map/bmk,bkn->bmn/dot_general | solution.py:17
  539.9 51.7 %fusion.3 = f32[1,8,1024,1024]{2,3,1,0:T(8,128)} fusion(f32[8,1024,1024]{2,1,0:T(8,128)} %fusion.23, f32[8,1024,1024]{2,1,0:T(8,128)} %fusion.26, f32[8,256,1024]{2,1,0:T(8,128)} %bitcast.147, f32[8,256,1024]{2,1,0:T(8,128)} %bitcast.149, f32[1,2,8,1024,256]{4,3,2,1,0:T(8,128)} %param.2), kind=kOutput, calls=%fused_computation.9 | convolution fusion | flops 25790775296 | bytes 134217728 | tf_op jit(solution)/shard_map/bmk,bkn->bmn/dot_general | solution.py:19
  591.6 33.0 %fusion.2 = f32[1,8,1024,1024]{2,3,1,0:T(8,128)} fusion(f32[8,1024,1024]{2,1,0:T(8,128)} %fusion.23, f32[8,1024,1024]{2,1,0:T(8,128)} %fusion.26), kind=kLoop, calls=%fused_computation.8 | loop fusion | flops 8388608 | bytes 100663296 | tf_op jit(solution)/shard_map/stack | solution.py:35
  624.6 23.5 %fusion = f32[2,8,1024,512]{2,3,1,0:T(8,128)} fusion(s32[]{:T(128)S(6)} %select_n.20, f32[1,8,1024,1024]{2,3,1,0:T(8,128)} %fusion.2, f32[1,8,1024,1024]{2,3,1,0:T(8,128)} %fusion.3), kind=kLoop, calls=%fused_computation.4 | loop fusion | flops 8388608 | bytes 100663296 | tf_op jit(solution)/shard_map/stack | solution.py:35
  648.1 0.0 collective-permute-start
  648.1 49.5 %collective-permute-done = f32[2,8,1024,512]{2,3,1,0:T(8,128)} collective-permute-done((f32[2,8,1024,512]{2,3,1,0:T(8,128)}, f32[2,8,1024,512]{2,3,1,0:T(8,128)}, u32[]{:S(2)}, u32[]{:S(2)}) %collective-permute-start) | collective-permute-done | bytes 33554464 | tf_op jit(solution)/shard_map/ppermute | solution.py:12
  697.6 56.2 %broadcast_select_fusion.1 = (f32[2,8,1024,512]{2,3,1,0:T(8,128)}, f32[2,8,1024,512]{2,3,1,0:T(8,128)}) fusion(f32[2,8,1024,512]{2,3,1,0:T(8,128)} %collective-permute-done, pred[]{:T(512)S(6)} %eq.3, s32[]{:T(128)S(6)} %select_n.19, f32[1,8,1024,1024]{2,3,1,0:T(8,128)} %fusion.3, f32[1,8,1024,1024]{2,3,1,0:T(8,128)} %fusion.2), kind=kLoop, calls=%fused_computation.24 | loop fusion | flops 33554432 | bytes 167772160 | tf_op jit(solution)/shard_map/jit(_where)/select_n | solution.py:42
  753.8 62.5 %fusion.7 = f32[1024,1024,1]{1,0,2:T(8,128)S(1)} fusion(f32[2,8,1024,512]{2,3,1,0:T(8,128)} %get-tuple-element.6, f32[2,8,1024,512]{2,3,1,0:T(8,128)} %get-tuple-element.5), kind=kOutput, calls=%fused_computation.14 | convolution fusion | flops 51539607552 | bytes 37748736 | tf_op jit(solution)/shard_map/bmn,bon->mo/dot_general | solution.py:18
  816.3 62.5 %fusion.10 = f32[1024,1024,1]{1,0,2:T(8,128)S(1)} fusion(f32[2,8,1024,512]{2,3,1,0:T(8,128)} %get-tuple-element.6, f32[2,8,1024,512]{2,3,1,0:T(8,128)} %get-tuple-element.5), kind=kOutput, calls=%fused_computation.17 | convolution fusion | flops 51539607552 | bytes 37748736 | tf_op jit(solution)/shard_map/bmn,bon->mo/dot_general | solution.py:17
  878.8 65.6 %fusion.34 = f32[1024,1,1024]{2,0,1:T(8,128)S(1)} fusion(f32[1024,1024,1]{1,0,2:T(8,128)S(1)} %fusion.7, f32[1024,1024,1]{1,0,2:T(8,128)S(1)} %fusion.10, f32[2,8,1024,512]{2,3,1,0:T(8,128)} %get-tuple-element.6, f32[2,8,1024,512]{2,3,1,0:T(8,128)} %get-tuple-element.5), kind=kOutput, calls=%fused_computation.47 | convolution fusion | flops 51550093312 | bytes 79691776 | tf_op jit(solution)/shard_map/bmn,bon->mo/dot_general | solution.py:19
  944.4 1.4 fusion.35
  945.8 4.3 maximum_multiply_fusion
  950.0 0.0 reduce-scatter.2.cloned.1.call-update
  950.0 102.6 %reduce-scatter.2.cloned.1.call-done = f32[64,2,1024]{2,0,1:T(8,128)} async-done(((f32[1024,2,1024]{2,0,1:T(8,128)}), f32[64,2,1024]{2,0,1:T(8,128)}) %reduce-scatter.2.cloned.1.call-update) | async-done | bytes 524304 | tf_op jit(solution)/shard_map/reduce_scatter | solution.py:48
  1052.6 2.2 copy.41
Async XLA Ops:
  6.5 13.9 %copy-start.2 = (f32[1,2,64,32,1024]{4,3,2,1,0:T(8,128)S(1)}, f32[1,2,64,32,1024]{4,3,2,1,0:T(8,128)}, u32[]{:S(2)}) copy-start(f32[1,2,64,32,1024]{4,3,2,1,0:T(8,128)} %param.3) | copy-start | bytes 50331652
  26.3 370.4 %all-to-all-start = ((f32[8,2,8,32,1024]{4,3,2,1,0:T(8,128)}), f32[8,2,8,32,1024]{4,3,2,1,0:T(8,128)}, u32[]{:S(2)}, u32[]{:S(2)}) async-start(f32[8,2,8,32,1024]{4,3,2,1,0:T(8,128)} %fusion.40), calls=%async_computation | async-start | bytes 33554432 | tf_op jit(solution)/shard_map/all_to_all | solution.py:30
  33.6 1019.1 %reduce-scatter.2.cloned.1.call-start = ((), (), s32[]{:S(2)}) async-start(), calls=%async_computation.2 | async-start | bytes 8912896 | tf_op jit(solution)/shard_map/reduce_scatter | solution.py:48
  415.2 63.1 %copy-start.1 = (f32[1,8,8,32,1024]{4,3,2,1,0:T(8,128)}, f32[1,8,8,32,1024]{4,3,2,1,0:T(8,128)S(1)}, u32[]{:S(2)}) copy-start(f32[1,8,8,32,1024]{4,3,2,1,0:T(8,128)S(1)} %get-tuple-element.8) | copy-start | bytes 25165828
  415.2 63.1 %copy-start = (f32[1,8,8,32,1024]{4,3,2,1,0:T(8,128)}, f32[1,8,8,32,1024]{4,3,2,1,0:T(8,128)S(1)}, u32[]{:S(2)}) copy-start(f32[1,8,8,32,1024]{4,3,2,1,0:T(8,128)S(1)} %get-tuple-element.7) | copy-start | bytes 25165828
  648.1 49.5 %collective-permute-start = (f32[2,8,1024,512]{2,3,1,0:T(8,128)}, f32[2,8,1024,512]{2,3,1,0:T(8,128)}, u32[]{:S(2)}, u32[]{:S(2)}) collective-permute-start(f32[2,8,1024,512]{2,3,1,0:T(8,128)} %fusion), channel_id=1, source_target_pairs={{0,1},{1,0},{2,3},{3,2},{4,5},{5,4},{6,7},{7,6},{8,9},{9,8},{10,11... | collective-permute-start | bytes 100663304 | tf_op jit(solution)/shard_map/ppermute | solution.py:12
Sparse Core Ops, SparseCore 0:
  950.2 102.4 reduce-scatter.1
